TPU v7x, 32 devices: a whole 2x2x4 slice. The times are simulated.
32 devices in a mesh: groups: 2 (over x), ctx: 4 (over y, core), heads: 4 (over z).
Axes of the slice: x: 2, y: 2, z: 4, core: 2. Of those that a mesh axis runs over, the one named last changes fastest.
Arguments:
- tokens: bfloat16 [4096, 2048], P(('groups', 'ctx', 'heads')), parts along dimension 0, may hold values from -60 to 60
- state_in: float32 [4, 256, 128], P('heads', 'groups'), parts along dimension 1, may hold values from -256 to 256
- past_kv: bfloat16 [2, 1024, 512], P(None, 'groups', 'heads'), parts along dimension 1, may hold values from -6 to 6
- w_qkv: bfloat16 [2048, 3, 512], P(None, None, 'heads'), may hold values from -0.125 to 0.125
- w_out: bfloat16 [512, 2048], P('heads'), may hold values from -0.25 to 0.25
- w_gate: bfloat16 [16, 2048, 768], P(('ctx', 'heads')), may hold values from -0.125 to 0.125
- w_up: bfloat16 [16, 2048, 768], P(('ctx', 'heads')), may hold values from -0.125 to 0.125
- w_down: bfloat16 [16, 768, 2048], P(('ctx', 'heads')), may hold values from -0.21875 to 0.21875
- expert_ids: int32 [4096, 8], P(('groups', 'ctx', 'heads')), parts along dimension 0, may hold values from 0 to 15, all different within a row; in each aligned block of 128 rows (0 to 127, 128 to 255, ...) at most 128 rows name the same one
- gate_weights: float32 [4096, 8], P(('groups', 'ctx', 'heads')), parts along dimension 0, may hold values from 0.1 to 1
Outputs:
- mixed: bfloat16 [4096, 2048], P(('groups', 'ctx', 'heads')), parts along dimension 0
There are 2 independent parts, one for each index of `groups`. A program takes and returns all parts, laid end to end along the dimension named above; an argument that names none is the same for every part. Nothing has to cross between parts.
Inputs may be any that keep to these rules, and one draw needn't show every extreme that they name: `expert_ids`: each row names 8 different experts; in each aligned block of 128 rows (the rows of one device) no expert is named by more than 128 rows, a bound that some block reaches.
All inputs are finite; a program needn't handle non-finite values.
Results may differ from a plain program's by a relative error of at most 0.017.
Values may be sent and summed in bfloat16 or wider, within the bound.
A program may use at most 128 MiB of HBM per device.

v0:
```python
import math
import jax
import jax.numpy as jnp
from jax import lax
from jax.sharding import PartitionSpec as P

HDIM = 128
WINDOW = 512


def entering(x, axis, join, neutral):
    place = lax.axis_index(axis)
    gathered = lax.all_gather(x.astype(jnp.bfloat16), axis)
    state = jnp.zeros_like(x) + jnp.asarray(neutral, x.dtype)

    def one(lap, state):
        return join(state, lax.dynamic_index_in_dim(gathered, lap, 0, False).astype(x.dtype))

    return lax.fori_loop(0, place, one, state)


def from_behind(block, axis, distance):
    devices = range(lax.axis_size(axis))
    route = [(i - distance, i) for i in devices if i - distance in devices]
    return lax.ppermute(block, axis, route)


def normalize(value):
    return value * lax.rsqrt(jnp.mean(value * value, axis=-1, keepdims=True) + 1e-06)


def dense_experts(
    hidden_float, normed, w_gate, w_up, w_down, expert_ids, gate_weights, expert_count
):
    axes = ("ctx", "heads")
    exp_local = w_gate.shape[0]
    chosen = expert_ids[:, :, None] == jnp.arange(expert_count, dtype=jnp.int32)
    table = jnp.sum(jnp.where(chosen, gate_weights[:, :, None], 0.0), axis=1)
    weights = lax.all_gather(table, axes, axis=0, tiled=True)
    first = lax.axis_index(axes) * exp_local
    rows = lax.all_gather(normed, axes, axis=0, tiled=True)
    total = None
    for e in range(exp_local):
        gate_act = jnp.dot(rows, w_gate[e], preferred_element_type=jnp.float32)
        up_act = jnp.dot(rows, w_up[e], preferred_element_type=jnp.float32)
        hid = (jax.nn.silu(gate_act) * up_act).astype(jnp.bfloat16)
        out_rows = jnp.dot(hid, w_down[e], preferred_element_type=jnp.float32)
        weight = lax.dynamic_slice_in_dim(weights, first + e, 1, 1)
        part = weight * out_rows
        total = part if total is None else total + part
    routed = lax.psum_scatter(total.astype(jnp.bfloat16), axes, scatter_dimension=0, tiled=True)
    return (hidden_float + routed.astype(jnp.float32)).astype(jnp.bfloat16)


def on_device(
    tokens, state_in, past_kv, w_qkv, w_out, w_gate, w_up, w_down, expert_ids, gate_weights
):
    row_count, model_width = tokens.shape
    inner_width = w_qkv.shape[2]
    local_heads = inner_width // HDIM
    w_flat = w_qkv.reshape(model_width, 3 * inner_width)
    projected = jnp.dot(
        lax.all_gather(tokens, "heads", axis=0, tiled=True),
        w_flat,
        preferred_element_type=jnp.float32,
    ).astype(jnp.bfloat16)
    slab_rows = projected.shape[0]
    projected = projected.reshape(slab_rows, 3, local_heads, HDIM)
    query = jnp.transpose(projected[:, 0], (1, 0, 2))
    keys = jnp.transpose(projected[:, 1], (1, 0, 2))
    values = jnp.transpose(projected[:, 2], (1, 0, 2))
    local_state = jnp.einsum("hsd,hse->hde", keys, values, preferred_element_type=jnp.float32)
    earlier_state = entering(
        local_state, "ctx", lambda first, second: first + second, jnp.zeros_like(local_state)
    )
    start_state = state_in + earlier_state
    tail = jnp.stack([keys, values], axis=0)
    arrived = from_behind(tail, "ctx", 1)
    past = jnp.transpose(past_kv.reshape(2, WINDOW, local_heads, HDIM), (0, 2, 1, 3))
    previous = jnp.where(lax.axis_index("ctx") == 0, past, arrived)
    all_keys = jnp.concatenate([previous[0], keys], axis=1)
    all_values = jnp.concatenate([previous[1], values], axis=1)
    block_rows = min(slab_rows, 512)
    block_count = slab_rows // block_rows
    scale = 1.0 / math.sqrt(HDIM)
    causal = jnp.arange(block_rows)[:, None] >= jnp.arange(block_rows)[None, :]
    offsets = jnp.arange(WINDOW + block_rows)[None, :] - jnp.arange(block_rows)[:, None]
    in_window = (offsets > 0) & (offsets <= WINDOW)

    def block_step(state, index):
        first = index * block_rows
        carried = jnp.einsum(
            "hsd,hde->hse", query.astype(jnp.float32), state, precision=lax.Precision.HIGHEST
        )
        inside = jnp.einsum("hsd,htd->hst", query, keys, preferred_element_type=jnp.float32)
        inside = jnp.where(causal[None], inside, 0.0).astype(jnp.bfloat16)
        linear = carried + jnp.einsum(
            "hst,hte->hse", inside, values, preferred_element_type=jnp.float32
        )
        scores = (
            jnp.einsum("hsd,htd->hst", query, all_keys, preferred_element_type=jnp.float32) * scale
        )
        scores = jnp.where(in_window[None], scores, -jnp.inf)
        top_score = jnp.max(scores, axis=-1, keepdims=True)
        expo = jnp.exp(scores - top_score)
        probs = (expo / jnp.sum(expo, axis=-1, keepdims=True)).astype(jnp.bfloat16)
        window_out = jnp.einsum(
            "hst,hte->hse", probs, all_values, preferred_element_type=jnp.float32
        )
        combined = (normalize(linear) + window_out).astype(jnp.bfloat16)
        new_state = state + jnp.einsum(
            "hsd,hse->hde", keys, values, preferred_element_type=jnp.float32
        )
        return (new_state, combined)

    _, outs = lax.scan(block_step, start_state, jnp.arange(block_count, dtype=jnp.int32))
    heads_out = jnp.transpose(outs, (0, 2, 1, 3)).reshape(slab_rows, inner_width)
    regrouped = lax.all_to_all(heads_out, "heads", split_axis=0, concat_axis=1, tiled=True)
    attn = jnp.dot(
        regrouped,
        lax.all_gather(w_out, "heads", axis=0, tiled=True),
        preferred_element_type=jnp.float32,
    )
    hidden_state = (tokens.astype(jnp.float32) + attn).astype(jnp.bfloat16)
    hidden_float = hidden_state.astype(jnp.float32)
    normed = normalize(hidden_float).astype(jnp.bfloat16)
    ctx_count = lax.axis_size("ctx")
    head_count = lax.axis_size("heads")
    exp_local = w_gate.shape[0]
    expert_count = exp_local * ctx_count * head_count
    top_count = expert_ids.shape[1]
    capacity = max(2, 2 * row_count * top_count // expert_count)
    devices = ctx_count * head_count
    if row_count * devices <= expert_count * capacity:
        return dense_experts(
            hidden_float, normed, w_gate, w_up, w_down, expert_ids, gate_weights, expert_count
        )
    picks = expert_ids.reshape(-1)
    onehot = (picks[:, None] == jnp.arange(expert_count, dtype=jnp.int32)[None, :]).astype(
        jnp.int32
    )
    earlier = jnp.cumsum(onehot, axis=0) - onehot
    slots = jnp.sum(onehot * earlier, axis=1)
    destination = picks * capacity + slots
    source_rows = jnp.arange(row_count * top_count, dtype=jnp.int32) // top_count
    outgoing = jnp.zeros((expert_count * capacity, model_width), jnp.bfloat16)
    outgoing = outgoing.at[destination].set(normed[source_rows])
    sendable = outgoing.reshape(expert_count, 1, capacity, model_width)
    arrived_rows = lax.all_to_all(
        sendable, ("ctx", "heads"), split_axis=0, concat_axis=1, tiled=True
    )
    e_count, n_count, c_count, d_count = arrived_rows.shape
    flat = arrived_rows.reshape(e_count, n_count * c_count, d_count)
    gate_act = jnp.einsum("erd,edf->erf", flat, w_gate, preferred_element_type=jnp.float32)
    up_act = jnp.einsum("erd,edf->erf", flat, w_up, preferred_element_type=jnp.float32)
    hid = (jax.nn.silu(gate_act) * up_act).astype(jnp.bfloat16)
    out_rows = jnp.einsum("erf,efd->erd", hid, w_down, preferred_element_type=jnp.float32)
    finished = out_rows.astype(jnp.bfloat16).reshape(e_count, n_count, c_count, d_count)
    returned = lax.all_to_all(finished, ("ctx", "heads"), split_axis=1, concat_axis=0, tiled=True)
    returned = returned.reshape(expert_count * capacity, model_width)
    picked = returned[destination].reshape(row_count, top_count, model_width).astype(jnp.float32)
    routed = jnp.sum(gate_weights[:, :, None] * picked, axis=1)
    return (hidden_float + routed).astype(jnp.bfloat16)


def solution(mesh):
    return jax.shard_map(
        on_device,
        mesh=mesh,
        in_specs=(
            P(("groups", "ctx", "heads"), None),
            P("heads", "groups", None),
            P(None, "groups", "heads"),
            P(None, None, "heads"),
            P("heads", None),
            P(("ctx", "heads"), None, None),
            P(("ctx", "heads"), None, None),
            P(("ctx", "heads"), None, None),
            P(("groups", "ctx", "heads"), None),
            P(("groups", "ctx", "heads"), None),
        ),
        out_specs=P(("groups", "ctx", "heads"), None),
        check_vma=False,
    )
```

profile of v0, /device:TPU:0, one launch (start us, length us, event | category | flops | bytes accessed | tf_op | source)
XLA Modules:
  0.0 328.5 jit_solution(8045174008604358506)
XLA Ops:
  6.5 0.7 all-gather.5.cloned.1.call-update
  7.3 0.7 all-gather.7.cloned.1.call-update
  8.0 2.6 copy.27
  10.6 46.7 %all-gather.5.cloned.1.call-done = bf16[512,2048]{1,0:T(8,128)(2,1)} async-done(((bf16[128,2048]{1,0:T(8,128)(2,1)}), bf16[512,2048]{1,0:T(8,128)(2,1)}) %all-gather.5.cloned.1.call-update) | async-done | bytes 2097168 | tf_op jit(solution)/shard_map/all_gather | solution.py:63
  57.3 3.1 convolution_convert_fusion
  60.4 0.2 convolution_convert_fusion.1
  60.6 0.7 fusion.38
  61.3 5.4 %all-gather = bf16[512,128]{1,0:T(8,128)(2,1)S(1)} all-gather(bf16[128,128]{1,0:T(8,128)(2,1)S(1)} %convolution_convert_fusion.1), channel_id=2, replica_groups=mesh['groups'=2,'ctx'=4,'heads'=4] {'ctx'}, dimensions={0}, use_global_device_ids=true | all-gather | bytes 163840 | tf_op jit(solution)/shard_map/all_gather | solution.py:13
  66.7 1.0 copy.35
  67.8 1.7 copy.34
  69.4 1.6 pad_maximum_fusion
  71.1 3.0 collective-permute-start
  74.0 2.0 fusion.26
  76.0 2.3 multiply_reduce_fusion.1
  78.3 1.1 bitcast_select_fusion
  79.4 1.5 fusion.39
  80.9 0.5 fusion.11
  81.5 0.6 fusion.15
  82.1 0.8 copy.33
  82.8 3.5 %all-to-all-start = ((bf16[4,128,128]{1,2,0:T(8,128)(2,1)}), bf16[4,128,128]{1,2,0:T(8,128)(2,1)S(1)}, u32[]{:S(2)}, u32[]{:S(2)}) async-start(bf16[4,128,128]{1,2,0:T(8,128)(2,1)} %copy.33), calls=%async_computation | async-start | bytes 262144 | tf_op jit(solution)/shard_map/all_to_all | solution.py:118
  86.3 0.0 all-gather.9.cloned.1.call-start
  86.3 19.8 %all-gather.7.cloned.1.call-done = bf16[512,2048]{1,0:T(8,128)(2,1)} async-done(((bf16[128,2048]{1,0:T(8,128)(2,1)}), bf16[512,2048]{1,0:T(8,128)(2,1)}) %all-gather.7.cloned.1.call-update) | async-done | bytes 2097168 | tf_op jit(solution)/shard_map/all_gather | solution.py:121
  106.2 2.2 multiply_reduce_fusion
  108.4 1.0 copy-done.1
  109.4 0.9 multiply_convert_fusion.2
  110.4 0.0 reduce-scatter.2.cloned.1.call-start
  110.5 33.1 %all_gather.22 = f32[2048,16]{0,1:T(8,128)S(1)} all-gather(f32[128,16]{0,1:T(8,128)S(1)} %select_reduce_fusion), channel_id=1, replica_groups=mesh['groups'=2,'ctx'=4,'heads'=4] {'ctx','heads'}, dimensions={0}, use_global_device_ids=true | all-gather | bytes 139264 | tf_op jit(solution)/shard_map/all_gather | solution.py:39
  143.6 41.7 %all-gather.9.cloned.1.call-done = bf16[2048,2048]{1,0:T(8,128)(2,1)} async-done(((bf16[128,2048]{1,0:T(8,128)(2,1)}), bf16[2048,2048]{1,0:T(8,128)(2,1)}) %all-gather.9.cloned.1.call-update) | async-done | bytes 8388624 | tf_op jit(solution)/shard_map/all_gather | solution.py:41
  185.3 11.7 %fusion.3 = f32[2048,768]{1,0:T(8,128)} fusion(bf16[2048,2048]{1,0:T(8,128)(2,1)} %all-gather.9.cloned.1.call-done, bf16[1,2048,768]{2,1,0:T(8,128)(2,1)} %param.17), kind=kOutput, calls=%fused_computation.5 | convolution fusion | flops 6442450944 | bytes 17825792 | tf_op jit(solution)/shard_map/dot_general | solution.py:44
  197.0 20.6 %multiply_convert_fusion = bf16[2048,2048]{1,0:T(8,128)(2,1)} fusion(f32[2048]{0:T(1024)S(1)} %bitcast.98, f32[2048,768]{1,0:T(8,128)} %fusion.3, bf16[2048,2048]{1,0:T(8,128)(2,1)} %all-gather.9.cloned.1.call-done, bf16[1,768,2048]{2,1,0:T(8,128)(2,1)S(1)} %copy-done, bf16[1,2048,768]{2,1,0:T(8,128)(2,1)} %param.18), kind=kOutput, calls=%fused_computation.1 | convolution fusion | flops 12902727680 | bytes 29368320 | tf_op jit(solution)/shard_map/dot_general | solution.py:47
  217.6 102.2 %reduce-scatter.2.cloned.1.call-done = bf16[128,2048]{1,0:T(8,128)(2,1)} async-done(((bf16[2048,2048]{1,0:T(8,128)(2,1)}), bf16[128,2048]{1,0:T(8,128)(2,1)}) %reduce-scatter.2.cloned.1.call-update) | async-done | bytes 524304 | tf_op jit(solution)/shard_map/reduce_scatter | solution.py:51
  319.7 2.3 add_convert_fusion
  (29 shorter events, 0.2 us)
Async XLA Ops:
  6.5 190.4 %copy-start = (bf16[1,768,2048]{2,1,0:T(8,128)(2,1)S(1)}, bf16[1,768,2048]{2,1,0:T(8,128)(2,1)}, u32[]{:S(2)}) copy-start(bf16[1,768,2048]{2,1,0:T(8,128)(2,1)} %param.19) | copy-start | bytes 9437188
  6.5 50.8 %all-gather.5.cloned.1.call-start = ((), (), s32[]{:S(2)}) async-start(), calls=%async_computation.2 | async-start | bytes 2621440 | tf_op jit(solution)/shard_map/all_gather | solution.py:63
  7.3 98.9 %all-gather.7.cloned.1.call-start = ((), (), s32[]{:S(2)}) async-start(), calls=%async_computation.3 | async-start | bytes 2621440 | tf_op jit(solution)/shard_map/all_gather | solution.py:121
  57.3 16.7 %copy-start.4 = (f32[1,128,128]{2,1,0:T(8,128)S(1)}, f32[1,128,128]{2,1,0:T(8,128)}, u32[]{:S(2)}) copy-start(f32[1,128,128]{2,1,0:T(8,128)} %param.13) | copy-start | bytes 196612
  60.4 6.3 %copy-start.3 = (bf16[512,384]{0,1:T(8,128)(2,1)}, bf16[512,384]{0,1:T(8,128)(2,1)S(1)}, u32[]{:S(2)}) copy-start(bf16[512,384]{0,1:T(8,128)(2,1)S(1)} %convolution_convert_fusion) | copy-start | bytes 1179652
  71.1 7.3 %collective-permute-start = (bf16[2,1,512,128]{3,2,1,0:T(8,128)(2,1)}, bf16[2,1,512,128]{3,2,1,0:T(8,128)(2,1)}, u32[]{:S(2)}, u32[]{:S(2)}) collective-permute-start(bf16[2,1,512,128]{3,2,1,0:T(8,128)(2,1)} %pad_maximum_fusion), channel_id=1, source_target_pairs={{0,4},{4,8},{8,12},{1,5},{5,9},{9,13},{2,6},{6,10},{10,14},{3,7},{... | collective-permute-start | bytes 786440 | tf_op jit(solution)/shard_map/ppermute | solution.py:25
  74.0 5.4 %copy-start.2 = (bf16[512,1,1,128]{3,0,2,1:T(8,128)(2,1)S(1)}, bf16[512,1,1,128]{3,0,2,1:T(8,128)(2,1)}, u32[]{:S(2)}) copy-start(bf16[512,1,1,128]{3,0,2,1:T(8,128)(2,1)} %copy.34) | copy-start | bytes 393220
  79.4 2.1 copy-start.7
  82.8 27.6 %copy-start.5 = (f32[128,8]{0,1:T(8,128)S(1)}, f32[128,8]{0,1:T(8,128)}, u32[]{:S(2)}) copy-start(f32[128,8]{0,1:T(8,128)} %param.21) | copy-start | bytes 12292
  82.8 27.6 %copy-start.6 = (s32[128,8]{0,1:T(8,128)S(1)}, s32[128,8]{0,1:T(8,128)}, u32[]{:S(2)}) copy-start(s32[128,8]{0,1:T(8,128)} %param.20) | copy-start | bytes 12292
  82.8 23.4 %all-to-all-start = ((bf16[4,128,128]{1,2,0:T(8,128)(2,1)}), bf16[4,128,128]{1,2,0:T(8,128)(2,1)S(1)}, u32[]{:S(2)}, u32[]{:S(2)}) async-start(bf16[4,128,128]{1,2,0:T(8,128)(2,1)} %copy.33), calls=%async_computation | async-start | bytes 262144 | tf_op jit(solution)/shard_map/all_to_all | solution.py:118
  86.3 99.0 %all-gather.9.cloned.1.call-start = ((), (), s32[]{:S(2)}) async-start(), calls=%async_computation.4 | async-start | bytes 8912896 | tf_op jit(solution)/shard_map/all_gather | solution.py:41
  108.4 1.0 copy-start.1
  110.4 209.4 %reduce-scatter.2.cloned.1.call-start = ((), (), s32[]{:S(2)}) async-start(), calls=%async_computation.5 | async-start | bytes 8912896 | tf_op jit(solution)/shard_map/reduce_scatter | solution.py:51
Sparse Core Ops, SparseCore 0:
  8.9 48.3 all-gather.4
  58.9 47.2 all-gather.6
  110.5 74.7 all-gather.8
  217.7 101.9 reduce-scatter.1
where the time goes:
time: 329 us
  waiting for transfers between devices  212 us (64%)
  matrix products  44.1 us (13%)
  blocking collectives  38.5 us (12%)
  between operations  13.3 us (4%)
  local copies, waits for them, and re-layouts  7.86 us (2%)
  starting transfers between devices  6.54 us (2%)
  other arithmetic  6.41 us (2%)
    reduce_scatter x1, waiting for transfers between devices, dense_experts(): lax.psum_scatter(total.astype(jnp.bfloat16), axes, scatter_dimension=0, t...  102 us
    all_gather x1, waiting for transfers between devices, on_device(): lax.all_gather(tokens, 'heads', axis=0, tiled=True)  46.7 us
    all_gather x1, waiting for transfers between devices, dense_experts(): rows = lax.all_gather(normed, axes, axis=0, tiled=True)  41.7 us
    all_gather x1, blocking collectives, dense_experts(): weights = lax.all_gather(table, axes, axis=0, tiled=True)  33.1 us
    dot_general x1, matrix products, dense_experts(): out_rows = jnp.dot(hid, w_down[e], preferred_element_type=jnp.float32)  20.6 us
    all_gather x1, waiting for transfers between devices, on_device(): lax.all_gather(w_out, 'heads', axis=0, tiled=True)  19.8 us
    dot_general x1, matrix products, dense_experts(): gate_act = jnp.dot(rows, w_gate[e], preferred_element_type=jnp.float32)  11.7 us
  transfers between devices with their start and end apart: 6, of which 4 were waited for; matrix products, arithmetic and copies ran while one was open for 6% of the time, Pallas kernels for 0%

commit v1 on v0

--- a/solution.py
+++ b/solution.py
@@ -6,6 +6,19 @@
 
 HDIM = 128
 WINDOW = 512
+
+
+def gather_around(x, axis, dim):
+    ways = lax.axis_size(axis)
+    up = [(d, (d + 1) % ways) for d in range(ways)]
+    down = [(d, (d - 1) % ways) for d in range(ways)]
+    earlier, later = ([x], [x])
+    for _ in range(ways // 2):
+        earlier.append(lax.ppermute(earlier[-1], axis, up))
+    for _ in range((ways - 1) // 2):
+        later.append(lax.ppermute(later[-1], axis, down))
+    line = jnp.concatenate([*earlier[::-1], *later[1:]], axis=dim)
+    return jnp.roll(line, (lax.axis_index(axis) - ways // 2) * x.shape[dim], axis=dim)
 
 
 def entering(x, axis, join, neutral):
@@ -60,9 +73,7 @@
     local_heads = inner_width // HDIM
     w_flat = w_qkv.reshape(model_width, 3 * inner_width)
     projected = jnp.dot(
-        lax.all_gather(tokens, "heads", axis=0, tiled=True),
-        w_flat,
-        preferred_element_type=jnp.float32,
+        gather_around(tokens, "heads", 0), w_flat, preferred_element_type=jnp.float32
     ).astype(jnp.bfloat16)
     slab_rows = projected.shape[0]
     projected = projected.reshape(slab_rows, 3, local_heads, HDIM)

time: 329 us -> 331 us (level)
  waiting for transfers between devices: 212 us -> 196 us
  blocking collectives: 38.5 us -> 46.7 us
  local copies, waits for them, and re-layouts: 7.86 us -> 14.9 us
  starting transfers between devices: 6.54 us -> 9.9 us
    ppermute x0 -> x3, waiting for transfers between devices: none -> 51.8 us  [the longest x2 26.9 us: gather_around(): earlier.append(lax.ppermute(earlier[-1], axis, up))]
    all_gather x1 -> x0, waiting for transfers between devices: 46.7 us -> none  [on_device(): lax.all_gather(tokens, 'heads', axis=0, tiled=True)]
    all_gather x1, waiting for transfers between devices: 19.8 us -> 0.01 us  [on_device(): lax.all_gather(w_out, 'heads', axis=0, tiled=True)]
    all_to_all x0 -> x1, blocking collectives: none -> 8.93 us  [on_device(): lax.all_to_all(heads_out, 'heads', split_axis=0, concat_axis=1, tiled=True)]
    ppermute x0 -> x3, starting transfers between devices: none -> 6.88 us  [the longest x1 3.82 us: gather_around(): later.append(lax.ppermute(later[-1], axis, down))]
    unnamed x19 -> x28, local copies, waits for them, and re-layouts: 6.34 us -> 12.9 us
    all_to_all x1 -> x0, starting transfers between devices: 3.46 us -> none  [on_device(): lax.all_to_all(heads_out, 'heads', split_axis=0, concat_axis=1, tiled=True)]
  transfers between devices with their start and end apart: 6 -> 7, of which waited for: 4 -> 5; matrix products, arithmetic and copies ran while one was open for 6% -> 7% of each run, Pallas kernels for 0% -> 0%
where the time goes in v1:
time: 331 us; the launch traced here: 330 us
  waiting for transfers between devices  196 us (59%)
  blocking collectives  46.7 us (14%)
  matrix products  42 us (13%)
  local copies, waits for them, and re-layouts  14.9 us (5%)
  between operations  13.4 us (4%)
  starting transfers between devices  9.9 us (3%)
  other arithmetic  6.44 us (2%)
    reduce_scatter x1, waiting for transfers between devices, dense_experts(): lax.psum_scatter(total.astype(jnp.bfloat16), axes, scatter_dimension=0, t...  102 us
    all_gather x1, waiting for transfers between devices, dense_experts(): rows = lax.all_gather(normed, axes, axis=0, tiled=True)  42.4 us
    all_gather x1, blocking collectives, dense_experts(): weights = lax.all_gather(table, axes, axis=0, tiled=True)  32.4 us
    ppermute x2, waiting for transfers between devices, gather_around(): earlier.append(lax.ppermute(earlier[-1], axis, up))  26.9 us
    ppermute x1, waiting for transfers between devices, gather_around(): later.append(lax.ppermute(later[-1], axis, down))  24.9 us
    dot_general x1, matrix products, dense_experts(): out_rows = jnp.dot(hid, w_down[e], preferred_element_type=jnp.float32)  20.6 us
    unnamed x28, local copies, waits for them, and re-layouts  12.9 us
    dot_general x1, matrix products, dense_experts(): gate_act = jnp.dot(rows, w_gate[e], preferred_element_type=jnp.float32)  11.7 us
  transfers between devices with their start and end apart: 7, of which 5 were waited for; matrix products, arithmetic and copies ran while one was open for 7% of the time, Pallas kernels for 0%

profile of v1, /device:TPU:0, one launch (start us, length us, event | category | flops | bytes accessed | tf_op | source)
XLA Modules:
  0.0 329.8 jit_solution(11132390045069970315)
XLA Ops:
  6.5 3.1 collective-permute-start
  9.6 14.3 %collective-permute-done = bf16[128,2048]{1,0:T(8,128)(2,1)} collective-permute-done((bf16[128,2048]{1,0:T(8,128)(2,1)}, bf16[128,2048]{1,0:T(8,128)(2,1)}, u32[]{:S(2)}, u32[]{:S(2)}) %collective-permute-start) | collective-permute-done | bytes 524320 | tf_op jit(solution)/shard_map/ppermute | solution.py:17
  23.9 3.8 %collective-permute-start.2 = (bf16[128,2048]{1,0:T(8,128)(2,1)}, bf16[128,2048]{1,0:T(8,128)(2,1)}, u32[]{:S(2)}, u32[]{:S(2)}) collective-permute-start(bf16[128,2048]{1,0:T(8,128)(2,1)} %param.12), channel_id=1, source_target_pairs={{0,3},{1,0},{2,1},{3,2},{4,7},{5,4},{6,5},{7,6},{8,11},{9,8},{10,9... | collective-permute-start | bytes 1572872 | tf_op jit(solution)/shard_map/ppermute | solution.py:19
  27.8 2.7 copy.27
  30.5 12.6 %collective-permute-done.1 = bf16[128,2048]{1,0:T(8,128)(2,1)} collective-permute-done((bf16[128,2048]{1,0:T(8,128)(2,1)}, bf16[128,2048]{1,0:T(8,128)(2,1)}, u32[]{:S(2)}, u32[]{:S(2)}) %collective-permute-start.1) | collective-permute-done | bytes 524320 | tf_op jit(solution)/shard_map/ppermute | solution.py:17
  43.1 1.1 constant_dynamic-update-slice_fusion.7
  44.2 1.1 constant_dynamic-update-slice_fusion.6
  45.3 1.1 constant_dynamic-update-slice_fusion.5
  46.4 24.9 %collective-permute-done.2 = bf16[128,2048]{1,0:T(8,128)(2,1)} collective-permute-done((bf16[128,2048]{1,0:T(8,128)(2,1)}, bf16[128,2048]{1,0:T(8,128)(2,1)}, u32[]{:S(2)}, u32[]{:S(2)}) %collective-permute-start.2) | collective-permute-done | bytes 524320 | tf_op jit(solution)/shard_map/ppermute | solution.py:19
  71.2 1.1 constant_dynamic-update-slice_fusion.4
  72.3 1.1 constant_dynamic-update-slice_fusion.3
  73.4 1.1 constant_dynamic-update-slice_fusion.2
  74.6 1.1 constant_dynamic-update-slice_fusion
  75.7 1.0 fusion.15
  77.6 5.4 %all-gather = bf16[512,128]{1,0:T(8,128)(2,1)S(1)} all-gather(bf16[128,128]{1,0:T(8,128)(2,1)S(1)} %convolution_convert_fusion), channel_id=2, replica_groups=mesh['groups'=2,'ctx'=4,'heads'=4] {'ctx'}, dimensions={0}, use_global_device_ids=true | all-gather | bytes 163840 | tf_op jit(solution)/shard_map/all_gather | solution.py:26
  83.0 1.0 copy.35
  84.1 1.7 copy.34
  85.7 1.6 pad_maximum_fusion
  87.3 2.9 collective-permute-start.3
  90.3 1.9 fusion.31
  92.2 2.3 multiply_reduce_fusion.1
  94.6 1.1 bitcast_select_fusion
  95.7 1.5 fusion.45
  98.5 8.9 %all_to_all.19 = bf16[4,128,128]{1,2,0:T(8,128)(2,1)S(1)} all-to-all(bf16[4,128,128]{1,2,0:T(8,128)(2,1)S(1)} %copy.33), channel_id=1, replica_groups=mesh['groups'=2,'ctx'=4,'heads'=4] {'heads'}, dimensions={0} | all-to-all | bytes 262144 | tf_op jit(solution)/shard_map/all_to_all | solution.py:129
  107.4 2.2 multiply_reduce_fusion
  109.7 1.0 copy-done.1
  111.7 32.4 %all_gather.18 = f32[2048,16]{0,1:T(8,128)S(1)} all-gather(f32[128,16]{0,1:T(8,128)S(1)} %select_reduce_fusion), channel_id=1, replica_groups=mesh['groups'=2,'ctx'=4,'heads'=4] {'ctx','heads'}, dimensions={0}, use_global_device_ids=true | all-gather | bytes 139264 | tf_op jit(solution)/shard_map/all_gather | solution.py:52
  144.1 42.4 %all-gather.6.cloned.1.call-done = bf16[2048,2048]{1,0:T(8,128)(2,1)} async-done(((bf16[128,2048]{1,0:T(8,128)(2,1)}), bf16[2048,2048]{1,0:T(8,128)(2,1)}) %all-gather.6.cloned.1.call-update) | async-done | bytes 8388624 | tf_op jit(solution)/shard_map/all_gather | solution.py:54
  186.5 11.7 %fusion.3 = f32[2048,768]{1,0:T(8,128)} fusion(bf16[2048,2048]{1,0:T(8,128)(2,1)} %all-gather.6.cloned.1.call-done, bf16[1,2048,768]{2,1,0:T(8,128)(2,1)} %param.17), kind=kOutput, calls=%fused_computation.5 | convolution fusion | flops 6442450944 | bytes 17825792 | tf_op jit(solution)/shard_map/dot_general | solution.py:57
  198.2 20.6 %multiply_convert_fusion = bf16[2048,2048]{1,0:T(8,128)(2,1)} fusion(f32[2048]{0:T(1024)S(1)} %bitcast.97, f32[2048,768]{1,0:T(8,128)} %fusion.3, bf16[2048,2048]{1,0:T(8,128)(2,1)} %all-gather.6.cloned.1.call-done, bf16[1,768,2048]{2,1,0:T(8,128)(2,1)S(1)} %copy-done, bf16[1,2048,768]{2,1,0:T(8,128)(2,1)} %param.18), kind=kOutput, calls=%fused_computation.1 | convolution fusion | flops 12902727680 | bytes 29368320 | tf_op jit(solution)/shard_map/dot_general | solution.py:60
  218.8 102.2 %reduce-scatter.2.cloned.1.call-done = bf16[128,2048]{1,0:T(8,128)(2,1)} async-done(((bf16[2048,2048]{1,0:T(8,128)(2,1)}), bf16[128,2048]{1,0:T(8,128)(2,1)}) %reduce-scatter.2.cloned.1.call-update) | async-done | bytes 524304 | tf_op jit(solution)/shard_map/reduce_scatter | solution.py:64
  321.0 2.3 add_convert_fusion
  (41 shorter events, 3.3 us)
Async XLA Ops:
  6.5 191.7 %copy-start = (bf16[1,768,2048]{2,1,0:T(8,128)(2,1)S(1)}, bf16[1,768,2048]{2,1,0:T(8,128)(2,1)}, u32[]{:S(2)}) copy-start(bf16[1,768,2048]{2,1,0:T(8,128)(2,1)} %param.19) | copy-start | bytes 9437188
  6.5 100.9 %all-gather.4.cloned.1.call-start = ((), (), s32[]{:S(2)}) async-start(), calls=%async_computation.2 | async-start | bytes 2621440 | tf_op jit(solution)/shard_map/all_gather | solution.py:132
  6.5 17.3 %collective-permute-start = (bf16[128,2048]{1,0:T(8,128)(2,1)}, bf16[128,2048]{1,0:T(8,128)(2,1)}, u32[]{:S(2)}, u32[]{:S(2)}) collective-permute-start(bf16[128,2048]{1,0:T(8,128)(2,1)} %param.12), channel_id=1, source_target_pairs={{0,1},{1,2},{2,3},{3,0},{4,5},{5,6},{6,7},{7,4},{8,9},{9,10},{10,1... | collective-permute-start | bytes 1572872 | tf_op jit(solution)/shard_map/ppermute | solution.py:17
  23.9 19.2 %collective-permute-start.1 = (bf16[128,2048]{1,0:T(8,128)(2,1)}, bf16[128,2048]{1,0:T(8,128)(2,1)}, u32[]{:S(2)}, u32[]{:S(2)}) collective-permute-start(bf16[128,2048]{1,0:T(8,128)(2,1)} %collective-permute-done), channel_id=1, source_target_pairs={{0,1},{1,2},{2,3},{3,0},{4,5},{5,6},{6,7},{7,4},{8,9},{9,10},{10,1... | collective-permute-start | bytes 1572872 | tf_op jit(solution)/shard_map/ppermute | solution.py:17
  23.9 47.4 %collective-permute-start.2 = (bf16[128,2048]{1,0:T(8,128)(2,1)}, bf16[128,2048]{1,0:T(8,128)(2,1)}, u32[]{:S(2)}, u32[]{:S(2)}) collective-permute-start(bf16[128,2048]{1,0:T(8,128)(2,1)} %param.12), channel_id=1, source_target_pairs={{0,3},{1,0},{2,1},{3,2},{4,7},{5,4},{6,5},{7,6},{8,11},{9,8},{10,9... | collective-permute-start | bytes 1572872 | tf_op jit(solution)/shard_map/ppermute | solution.py:19
  27.7 158.8 %all-gather.6.cloned.1.call-start = ((), (), s32[]{:S(2)}) async-start(), calls=%async_computation.3 | async-start | bytes 8912896 | tf_op jit(solution)/shard_map/all_gather | solution.py:54
  30.4 44.1 %copy-start.2 = (bf16[128,2048]{1,0:T(8,128)(2,1)S(1)}, bf16[128,2048]{1,0:T(8,128)(2,1)}, u32[]{:S(2)}) copy-start(bf16[128,2048]{1,0:T(8,128)(2,1)} %param.12) | copy-start | bytes 1572868
  30.4 45.2 %copy-start.3 = (bf16[2048,3,128]{0,2,1:T(8,128)(2,1)S(1)}, bf16[2048,3,128]{0,2,1:T(8,128)(2,1)}, u32[]{:S(2)}) copy-start(bf16[2048,3,128]{0,2,1:T(8,128)(2,1)} %copy.27) | copy-start | bytes 4718596
  75.7 14.6 %copy-start.5 = (f32[1,128,128]{2,1,0:T(8,128)S(1)}, f32[1,128,128]{2,1,0:T(8,128)}, u32[]{:S(2)}) copy-start(f32[1,128,128]{2,1,0:T(8,128)} %param.13) | copy-start | bytes 196612
  76.7 6.3 %copy-start.4 = (bf16[512,384]{0,1:T(8,128)(2,1)}, bf16[512,384]{0,1:T(8,128)(2,1)S(1)}, u32[]{:S(2)}) copy-start(bf16[512,384]{0,1:T(8,128)(2,1)S(1)} %fusion.15) | copy-start | bytes 1179652
  87.3 7.2 %collective-permute-start.3 = (bf16[2,1,512,128]{3,2,1,0:T(8,128)(2,1)}, bf16[2,1,512,128]{3,2,1,0:T(8,128)(2,1)}, u32[]{:S(2)}, u32[]{:S(2)}) collective-permute-start(bf16[2,1,512,128]{3,2,1,0:T(8,128)(2,1)} %pad_maximum_fusion), channel_id=1, source_target_pairs={{0,4},{4,8},{8,12},{1,5},{5,9},{9,13},{2,6},{6,10},{10,14},{3,7},{... | collective-permute-start | bytes 786440 | tf_op jit(solution)/shard_map/ppermute | solution.py:38
  94.5 3.2 copy-start.8
  98.3 13.3 %copy-start.6 = (f32[128,8]{0,1:T(8,128)S(1)}, f32[128,8]{0,1:T(8,128)}, u32[]{:S(2)}) copy-start(f32[128,8]{0,1:T(8,128)} %param.21) | copy-start | bytes 12292
  98.3 13.3 %copy-start.7 = (s32[128,8]{0,1:T(8,128)S(1)}, s32[128,8]{0,1:T(8,128)}, u32[]{:S(2)}) copy-start(s32[128,8]{0,1:T(8,128)} %param.20) | copy-start | bytes 12292
  109.6 1.0 copy-start.1
  111.6 209.4 %reduce-scatter.2.cloned.1.call-start = ((), (), s32[]{:S(2)}) async-start(), calls=%async_computation.4 | async-start | bytes 8912896 | tf_op jit(solution)/shard_map/reduce_scatter | solution.py:64
Sparse Core Ops, SparseCore 0:
  27.8 54.5 all-gather.3
  111.7 74.7 all-gather.5
  218.9 102.0 reduce-scatter.1
